TPU v7x, 32 devices: a whole 2x2x4 slice. The times are simulated.
32 devices in a mesh: seq: 2 (over x), row: 16 (over z, y, core).
Axes of the slice: x: 2, y: 2, z: 4, core: 2. Of those that a mesh axis runs over, the one named last changes fastest.
Arguments:
- qm: float32 [2, 16, 7, 256, 256], P('seq', 'row'), parts along dimension 0, may hold values from 0.005 to 0.05
- qm1: float32 [2, 16, 7, 256, 256], P('seq', 'row'), parts along dimension 0, may hold values from 0.005 to 0.05
- qb: float32 [2, 16, 7, 256, 256], P('seq', 'row'), parts along dimension 0, may hold values from 0.05 to 2
- codes: int32 [2, 16, 256], P('seq', 'row'), parts along dimension 0, may hold values from 0 to 3
- energy_index: int32 [2, 16, 256, 256], P('seq', 'row'), parts along dimension 0, may hold values from 0 to 63
- turner: float32 [64], replicated, may hold values from -1 to 1.5
Outputs:
- qb_new: float32 [2, 16, 256, 256], P('seq', 'row'), parts along dimension 0
- qm1_new: float32 [2, 16, 256, 256], P('seq', 'row'), parts along dimension 0
- qm_new: float32 [2, 16, 256, 256], P('seq', 'row'), parts along dimension 0
There are 2 independent parts, one for each index of `seq`. A program takes and returns all parts, laid end to end along the dimension named above; an argument that names none is the same for every part. Nothing has to cross between parts.
All inputs are finite; a program needn't handle non-finite values.
Results may differ from a plain program's by a relative error of at most 0.0003.
Values sent between devices are 32-bit elements; how exact they have to be, the bound alone decides.
A program may use at most 64 MiB of HBM per device.

v0:
```python
import jax
import jax.numpy as jnp
import numpy as np
from jax import lax
from jax.sharding import PartitionSpec as P

B = 256
DIST = 8


PAIRS = np.array([[0, 0, 0, 1], [0, 0, 1, 0], [0, 1, 0, 1], [1, 0, 1, 0]], dtype=np.float32)
HI = lax.Precision.HIGHEST


def shifted(block, axis, distance):
    devices = range(lax.axis_size(axis))
    route = [((i - distance) % len(devices), i) for i in devices]
    return lax.ppermute(block, axis, route)


def unpaired(shift):
    offsets = jnp.arange(B, dtype=jnp.int32)
    diffs = (shift * B + offsets[None, :] - offsets[:, None]).astype(jnp.float32)
    values = 0.01 * jnp.exp(-diffs / (DIST * B))
    if shift == 0:
        values = jnp.where(diffs >= 0, values, jnp.float32(0.0))
    return values


def decay(level):
    offsets = jnp.arange(B, dtype=jnp.int32)
    diffs = ((DIST - level) * B + offsets[None, :] - offsets[:, None]).astype(jnp.float32)
    values = jnp.exp(-diffs / (DIST * B))
    if level == DIST:
        values = jnp.where(diffs >= 0, values, jnp.float32(0.0))
    return values


def pairing(first, second):
    table = jnp.asarray(PAIRS, dtype=jnp.float32)
    digits = jnp.arange(4, dtype=jnp.int32)
    left = (first[:, None] == digits[None, :]).astype(jnp.float32)
    right = (second[:, None] == digits[None, :]).astype(jnp.float32)
    return jnp.dot(jnp.dot(left, table, precision=HI), right.T, precision=HI)


def per_device(qm, qm1, qb, codes, energy_index, turner):
    width = lax.axis_size("row")
    myself = lax.axis_index("row")
    cycles = qm.shape[0]
    qm = qm[:, 0]
    qm1 = qm1[:, 0]
    qb = qb[:, 0]
    codes = codes[:, 0]
    energy_index = energy_index[:, 0]
    beta = 1.0 / (DIST * B)

    def advance(received, step):
        later = jnp.concatenate([received[1:], jnp.zeros_like(received)], 0)
        return jnp.where(myself + step >= width, later, received)

    rights = []
    for shift in range(1, DIST):
        piece = shifted(qm1[:, DIST - shift - 1], "row", -shift)
        rights.append(advance(piece, shift))
    ends = advance(shifted(codes, "row", -DIST), DIST)
    start_tail = unpaired(0)
    closing_decay = decay(DIST)
    live = 0 + myself + DIST < cycles * width
    allowed = pairing(codes[0], ends[0])
    weight = jnp.exp(-jnp.take(turner, energy_index[0]))
    summed = jnp.zeros((B, B), jnp.float32)
    for shift in range(1, DIST):
        summed = summed + jnp.dot(qm[0, shift - 1], rights[shift - 1][0], precision=HI)
    pair_new = allowed * weight * (1.0 + 0.8 * summed)
    branch = jnp.dot(pair_new, closing_decay, precision=HI)
    tails = jnp.zeros((B, B), jnp.float32)
    for shift in range(1, DIST):
        tails = tails + jnp.dot(unpaired(shift), rights[shift - 1][0], precision=HI)
    for level in range(1, DIST):
        branch = branch + jnp.dot(qb[0, level - 1], decay(level), precision=HI)
    branch = branch * beta
    multi = summed + tails + jnp.dot(start_tail, branch, precision=HI)
    zero = jnp.float32(0.0)
    pair_out = [jnp.where(live, pair_new, zero)]
    branch_out = [jnp.where(live, branch, zero)]
    multi_out = [jnp.where(live, multi, zero)]
    return (
        jnp.stack(pair_out, 0)[:, None],
        jnp.stack(branch_out, 0)[:, None],
        jnp.stack(multi_out, 0)[:, None],
    )


def solution(mesh):
    return jax.shard_map(
        per_device,
        mesh=mesh,
        in_specs=(
            P("seq", "row", None, None, None),
            P("seq", "row", None, None, None),
            P("seq", "row", None, None, None),
            P("seq", "row", None),
            P("seq", "row", None, None),
            P(),
        ),
        out_specs=(
            P("seq", "row", None, None),
            P("seq", "row", None, None),
            P("seq", "row", None, None),
        ),
        check_vma=False,
    )
```

profile of v0, /device:TPU:13, one launch (start us, length us, event | category | flops | bytes accessed | tf_op | source)
XLA Modules:
  0.0 712.0 jit_solution(10599824790510033032)
XLA Ops:
  0.7 2.7 slice_bitcast_fusion.34
  3.4 3.9 collective-permute-start.6
  7.7 0.7 collective-permute-start.4
  8.4 1.4 collective-permute-start
  9.8 0.6 iota_add_fusion.6
  10.4 0.6 iota_add_fusion.5
  11.0 0.6 iota_add_fusion.4
  11.6 0.6 iota_add_fusion.3
  12.4 0.9 fusion.131
  13.4 668.8 %gather_fusion = f32[65536]{0:T(1024)} fusion(f32[64]{0:T(128)S(1)} %copy-done, s32[65536]{0:T(1024)S(1)} %broadcast_clamp_fusion), kind=kCustom, calls=%fused_computation | custom fusion | bytes 786432 | tf_op jit(solution)/shard_map/jit(_take)/gather | solution.py:71
  682.2 1.0 reshape.78
  683.2 3.0 collective-permute-start.3
  686.3 0.7 broadcast_select_fusion
  686.9 0.8 collective-permute-start.2
  689.7 2.2 collective-permute-done.3
  692.3 6.9 collective-permute-done.2
  699.7 2.6 collective-permute-done.1
  703.1 0.4 fusion.61
  703.6 0.4 fusion.8
  704.5 0.4 fusion.6
  705.4 0.4 fusion.4
  706.8 0.5 fusion.51
  707.2 0.8 select_bitcast_fusion
  710.8 1.2 fusion.23
  (50 shorter events, 8.5 us)
Async XLA Ops:
  0.6 12.7 %copy-start = (f32[64]{0:T(128)S(1)}, f32[64]{0:T(128)}, u32[]{:S(2)}) copy-start(f32[64]{0:T(128)} %param.12) | copy-start | bytes 772
  0.6 11.5 %copy-start.3 = (s32[1,1,256,256]{3,2,1,0:T(8,128)S(1)}, s32[1,1,256,256]{3,2,1,0:T(8,128)}, u32[]{:S(2)}) copy-start(s32[1,1,256,256]{3,2,1,0:T(8,128)} %param.11) | copy-start | bytes 786436
  0.7 11.7 %copy-start.8 = (f32[4,4]{1,0:T(4,128)S(1)}, f32[4,4]{1,0:T(4,128)}, u32[]{:S(2)}) copy-start(f32[4,4]{1,0:T(4,128)} %constant.76.clone) | copy-start | bytes 196
  3.4 683.6 %collective-permute-start.7 = (f32[1,256,256]{2,1,0:T(8,128)}, f32[1,256,256]{2,1,0:T(8,128)S(1)}, u32[]{:S(2)}, u32[]{:S(2)}) collective-permute-start(f32[1,256,256]{2,1,0:T(8,128)} %get-tuple-element.4), channel_id=1, source_target_pairs={{7,0},{8,1},{9,2},{10,3},{11,4},{12,5},{13,6},{14,7},{15,8},{0,9},... | collective-permute-start | bytes 786440 | tf_op jit(solution)/shard_map/ppermute | solution.py:18
  3.4 684.8 %collective-permute-start.6 = (f32[1,256,256]{2,1,0:T(8,128)}, f32[1,256,256]{2,1,0:T(8,128)S(1)}, u32[]{:S(2)}, u32[]{:S(2)}) collective-permute-start(f32[1,256,256]{2,1,0:T(8,128)} %get-tuple-element.5), channel_id=1, source_target_pairs={{6,0},{7,1},{8,2},{9,3},{10,4},{11,5},{12,6},{13,7},{14,8},{15,9},... | collective-permute-start | bytes 786440 | tf_op jit(solution)/shard_map/ppermute | solution.py:18
  7.3 681.5 %collective-permute-start.5 = (f32[1,256,256]{2,1,0:T(8,128)}, f32[1,256,256]{2,1,0:T(8,128)S(1)}, u32[]{:S(2)}, u32[]{:S(2)}) collective-permute-start(f32[1,256,256]{2,1,0:T(8,128)} %get-tuple-element.6), channel_id=1, source_target_pairs={{5,0},{6,1},{7,2},{8,3},{9,4},{10,5},{11,6},{12,7},{13,8},{14,9},{... | collective-permute-start | bytes 786440 | tf_op jit(solution)/shard_map/ppermute | solution.py:18
  7.7 681.6 %collective-permute-start.4 = (f32[1,256,256]{2,1,0:T(8,128)}, f32[1,256,256]{2,1,0:T(8,128)S(1)}, u32[]{:S(2)}, u32[]{:S(2)}) collective-permute-start(f32[1,256,256]{2,1,0:T(8,128)} %get-tuple-element.7), channel_id=1, source_target_pairs={{4,0},{5,1},{6,2},{7,3},{8,4},{9,5},{10,6},{11,7},{12,8},{13,9},{1... | collective-permute-start | bytes 786440 | tf_op jit(solution)/shard_map/ppermute | solution.py:18
  8.4 674.9 %collective-permute-start = (s32[1,256]{1,0:T(1,128)}, s32[1,256]{1,0:T(1,128)}, u32[]{:S(2)}, u32[]{:S(2)}) collective-permute-start(s32[1,256]{1,0:T(1,128)} %bitcast.1), channel_id=1, source_target_pairs={{8,0},{9,1},{10,2},{11,3},{12,4},{13,5},{14,6},{15,7},{0,8},{1,9},... | collective-permute-start | bytes 3080 | tf_op jit(solution)/shard_map/ppermute | solution.py:18
  13.4 674.4 %copy-start.2 = (f32[1,1,7,256,256]{4,3,2,1,0:T(8,128)S(1)}, f32[1,1,7,256,256]{4,3,2,1,0:T(8,128)}, u32[]{:S(2)}) copy-start(f32[1,1,7,256,256]{4,3,2,1,0:T(8,128)} %param.7) | copy-start | bytes 5505028
  683.2 8.7 %collective-permute-start.3 = (f32[1,256,256]{2,1,0:T(8,128)}, f32[1,256,256]{2,1,0:T(8,128)S(1)}, u32[]{:S(2)}, u32[]{:S(2)}) collective-permute-start(f32[1,256,256]{2,1,0:T(8,128)} %get-tuple-element.8), channel_id=1, source_target_pairs={{3,0},{4,1},{5,2},{6,3},{7,4},{8,5},{9,6},{10,7},{11,8},{12,9},{13... | collective-permute-start | bytes 786440 | tf_op jit(solution)/shard_map/ppermute | solution.py:18
  686.9 12.3 %collective-permute-start.2 = (f32[1,256,256]{2,1,0:T(8,128)}, f32[1,256,256]{2,1,0:T(8,128)S(1)}, u32[]{:S(2)}, u32[]{:S(2)}) collective-permute-start(f32[1,256,256]{2,1,0:T(8,128)} %get-tuple-element.9), channel_id=1, source_target_pairs={{2,0},{3,1},{4,2},{5,3},{6,4},{7,5},{8,6},{9,7},{10,8},{11,9},{12,... | collective-permute-start | bytes 786440 | tf_op jit(solution)/shard_map/ppermute | solution.py:18
  688.2 14.1 %collective-permute-start.1 = (f32[1,256,256]{2,1,0:T(8,128)}, f32[1,256,256]{2,1,0:T(8,128)S(1)}, u32[]{:S(2)}, u32[]{:S(2)}) collective-permute-start(f32[1,256,256]{2,1,0:T(8,128)} %get-tuple-element.3), channel_id=1, source_target_pairs={{1,0},{2,1},{3,2},{4,3},{5,4},{6,5},{7,6},{8,7},{9,8},{10,9},{11,1... | collective-permute-start | bytes 786440 | tf_op jit(solution)/shard_map/ppermute | solution.py:18
  699.6 3.9 copy-start.1
  699.7 3.9 copy-start.7
  702.7 1.3 copy-start.6
  702.7 1.8 copy-start.5
  702.7 2.2 copy-start.4
where the time goes:
time: 713 us; the launch traced here: 712 us
  local copies, waits for them, and re-layouts  673 us (94%)
  matrix products  12 us (2%)
  waiting for transfers between devices  11.8 us (2%)
  starting transfers between devices  10.5 us (1%)
    gather x2, local copies, waits for them, and re-layouts, per_device(): weight = jnp.exp(-jnp.take(turner, energy_index[0]))  670 us
  transfers between devices with their start and end apart: 8, of which 3 were waited for; matrix products, arithmetic and copies ran while one was open for 95% of the time, Pallas kernels for 0%

commit v1 on v0

v1 whole, which is shorter than its diff:
```python
import functools

import jax
import jax.numpy as jnp
from jax import lax
from jax.experimental import pallas as pl
from jax.experimental.pallas import tpu as pltpu
from jax.sharding import PartitionSpec as P

F32 = jnp.float32
BF16 = jnp.bfloat16

PLAN = {
    1: (4, (3, 4, 5, 6, 7)),
    3: (6, (1, 2, 3, 4, 5, 6, 7)),
    4: (8, (4, 5, 6)),
    5: (9, (3, 4, 5, 6, 7)),
    6: (14, (3, 6, 7)),
    7: (10, (1, 2, 3, 5, 6)),
}


def split(x):
    high = x.astype(BF16)
    return high, (x - high.astype(F32)).astype(BF16)


def mm(a, b):
    return jnp.dot(a, b, preferred_element_type=F32)


def dot3(a, b):
    ah, al = a
    bh, bl = b
    return mm(ah, bh) + (mm(ah, bl) + mm(al, bh))


def any_of(x, values):
    hit = x == values[0]
    for value in values[1:]:
        hit = jnp.logical_or(hit, x == value)
    return hit


def kernel(
    plan, width, qm, qm1, qb, eidx, codes, turner, pair_out, branch_out, multi_out,
    q_own, r_own, q_far, r_far, qb_in, e_in, code_in, acc, acc_far, partial_in, weight, row_sum,
    tri_h, tri_l, up_h, up_l,
    own_sem, q_send, q_recv, r_send, r_recv, rf_recv, load_sem, code_sem, part_sem,
):
    dm, block = qm.shape[0], qm.shape[1]
    dist = dm + 1
    live_rows = width - dist
    beta = 1.0 / (dist * block)
    me = lax.axis_index("row")
    live = me < live_rows

    def remote(src, dst, send, recv, device):
        return pltpu.make_async_remote_copy(
            src_ref=src, dst_ref=dst, send_sem=send, recv_sem=recv,
            device_id={"row": device}, device_id_type=pl.DeviceIdType.MESH,
        )

    def moved_rows(m):
        return [row for row, (_, shifts) in plan.items() if m in shifts]

    def own(m):
        rows = moved_rows(m)
        return jnp.logical_and(live, jnp.logical_not(any_of(me, rows))) if rows else live

    def direct(m):
        row = me - m
        ok = jnp.logical_and(row >= 0, row < live_rows)
        rows = moved_rows(m)
        return jnp.logical_and(ok, jnp.logical_not(any_of(row, rows))) if rows else ok

    def code_send():
        return remote(codes, code_in, code_sem.at[0], code_sem.at[1], me - dist)

    def q_copy(m, device):
        return remote(qm.at[m - 1], q_far.at[m - 1], q_send.at[m - 1], q_recv.at[m - 1], device)

    def r_copy(m, device):
        return remote(qm1.at[dm - m], r_own.at[m - 1], r_send.at[m - 1], r_recv.at[m - 1], device)

    def rf_copy(m, device):
        return remote(qm1.at[dm - m], r_far.at[m - 1], r_send.at[m - 1], rf_recv.at[m - 1], device)

    def part_copy(device):
        return remote(acc_far, partial_in, part_sem.at[0], part_sem.at[1], device)

    for m in range(1, dist):
        for row in moved_rows(m):
            device = plan[row][0]

            @pl.when(me == row)
            def _():
                q_copy(m, device).start()

            if row + m == device:

                @pl.when(me == device)
                def _():
                    pltpu.make_async_copy(qm1.at[dm - m], r_far.at[m - 1], rf_recv.at[m - 1]).start()

            else:

                @pl.when(me == row + m)
                def _():
                    rf_copy(m, device).start()

    for m in range(1, dist):

        @pl.when(direct(m))
        def _():
            r_copy(m, me - m).start()

    @pl.when(me >= dist)
    def _():
        code_send().start()

    loads = (
        pltpu.make_async_copy(qb, qb_in, load_sem.at[0]),
        pltpu.make_async_copy(eidx, e_in, load_sem.at[1]),
    )

    @pl.when(live)
    def _():
        for load in loads:
            load.start()

    for m in range(1, dist):

        @pl.when(own(m))
        def _():
            pltpu.make_async_copy(qm.at[m - 1], q_own.at[m - 1], own_sem.at[m - 1]).start()

    acc[...] = jnp.zeros_like(acc)
    acc_far[...] = jnp.zeros_like(acc_far)
    rows_i = lax.broadcasted_iota(jnp.int32, (block, block), 0)
    cols_i = lax.broadcasted_iota(jnp.int32, (block, block), 1)
    column = lax.broadcasted_iota(jnp.int32, (block, 1), 0)
    line = lax.broadcasted_iota(jnp.int32, (1, block), 1)

    @pl.when(live)
    def _():
        diff = (cols_i - rows_i).astype(F32)
        fall = jnp.where(diff >= 0, jnp.exp(diff * (-beta)), 0.0)
        tri_h[...], tri_l[...] = split(fall)
        up_h[...], up_l[...] = split(0.01 * fall)
        code_send().wait_recv()
        first = jnp.sum(jnp.where(rows_i == cols_i, codes[...].astype(F32), 0.0), axis=1, keepdims=True)
        both = first + code_in[...].astype(F32)
        allowed = jnp.where(jnp.logical_or(both == 3.0, both == 5.0), 1.0, 0.0)
        table = jnp.exp(-turner[...])
        entries = table.shape[1]
        table = jnp.concatenate([table, jnp.zeros((1, 128 - entries), F32)], axis=1)
        table = jnp.broadcast_to(table, (block, 128))
        loads[1].wait()
        for start in range(0, block, 128):
            part = pl.ds(start, 128)
            found = jnp.take_along_axis(table, e_in[:, part], axis=1, mode="promise_in_bounds")
            weight[:, part] = found * allowed[:, start : start + 128]
        loads[0].wait()
        total = jnp.zeros((block, block), F32)
        for e in range(1, dist):
            factor = jnp.exp((line - (dist - e) * block).astype(F32) * beta)
            total = total + qb_in[e - 1] * factor
        row_sum[...] = jnp.broadcast_to(jnp.sum(total, axis=1, keepdims=True), row_sum.shape)

    def product(m, q, r, total):
        right = r[m]
        total[0:block, :] += dot3(split(q[m]), split(right))
        fade = jnp.exp((-(m + 1) * block - column).astype(F32) * beta)
        total[block : block + 1, :] += jnp.sum(right * fade, axis=0, keepdims=True)

    def mask_of(cases):
        total = jnp.int32(0)
        for device, shifts in cases:
            total = total + jnp.where(me == device, sum(2 ** (m - 1) for m in shifts), 0)
        return total

    if plan:
        far_mask = mask_of(list(plan.values()))

        def far_step(m, rest):
            @pl.when(rest % 2 == 1)
            def _():
                q_copy(m + 1, 0).wait_recv()
                rf_copy(m + 1, 0).wait_recv()
                product(m, q_far, r_far, acc_far)

            return rest // 2

        lax.fori_loop(0, dm, far_step, far_mask)
        for row, (device, _) in plan.items():

            @pl.when(me == device)
            def _():
                part_copy(row).start()

    moved = mask_of([(row, shifts) for row, (_, shifts) in plan.items()])
    own_mask = jnp.where(live, 2**dm - 1 - moved, 0)

    def own_step(m, rest):
        @pl.when(rest % 2 == 1)
        def _():
            pltpu.make_async_copy(qm.at[m], q_own.at[m], own_sem.at[m]).wait()
            r_copy(m + 1, 0).wait_recv()
            product(m, q_own, r_own, acc)

        return rest // 2

    lax.fori_loop(0, dm, own_step, own_mask)

    if plan:

        @pl.when(any_of(me, list(plan)))
        def _():
            part_copy(0).wait_recv()
            acc[...] += partial_in[...]

    @pl.when(live)
    def _():
        summed = acc[0:block, :]
        pair = weight[...] * (1.0 + 0.8 * summed)
        pair_out[...] = pair
        outer = row_sum[:, 0:1] * jnp.exp(line.astype(F32) * (-beta))
        branch = (outer + dot3(split(pair), (tri_h[...], tri_l[...]))) * beta
        branch_out[...] = branch
        tails = 0.01 * jnp.exp(column.astype(F32) * beta) * acc[block : block + 1, :]
        multi_out[...] = summed + tails + dot3((up_h[...], up_l[...]), split(branch))

    @pl.when(jnp.logical_not(live))
    def _():
        for out in (pair_out, branch_out, multi_out):
            out[...] = jnp.zeros_like(out)

    for m in range(1, dist):
        rows = moved_rows(m)
        row = me - m

        @pl.when(jnp.logical_and(row >= 0, row < live_rows))
        def _():
            if rows and any(plan[r][0] == r + m for r in rows):
                stays = any_of(me, [r + m for r in rows if plan[r][0] == r + m])

                @pl.when(jnp.logical_not(stays))
                def _():
                    r_copy(m, 0).wait_send()

            else:
                r_copy(m, 0).wait_send()

        if rows:

            @pl.when(any_of(me, rows))
            def _():
                q_copy(m, 0).wait_send()

    @pl.when(me >= dist)
    def _():
        code_send().wait_send()

    if plan:

        @pl.when(any_of(me, [device for device, _ in plan.values()]))
        def _():
            part_copy(0).wait_send()


def solution(mesh):
    width = mesh.shape["row"]

    def per_device(qm, qm1, qb, codes, energy_index, turner):
        dm, block = qm.shape[2], qm.shape[3]
        dist = dm + 1
        plan = PLAN if width == 16 and dist == 8 else {}
        blocks = pltpu.VMEM((dm, block, block), F32)
        whole = pltpu.VMEM((block, block), F32)
        half = pltpu.VMEM((block, block), BF16)
        tall = pltpu.VMEM((block + 8, block), F32)
        dma = pltpu.SemaphoreType.DMA
        anywhere = pl.BlockSpec(memory_space=pl.ANY)
        local = pl.BlockSpec(memory_space=pltpu.VMEM)
        outs = pl.pallas_call(
            functools.partial(kernel, plan, width),
            out_shape=[jax.ShapeDtypeStruct((block, block), F32)] * 3,
            in_specs=[anywhere] * 4 + [local] * 2,
            out_specs=[local] * 3,
            scratch_shapes=[
                blocks, blocks, blocks, blocks, blocks,
                pltpu.VMEM((block, block), jnp.int32),
                pltpu.VMEM((1, block), jnp.int32),
                tall, tall, tall, whole,
                pltpu.VMEM((block, 128), F32),
                half, half, half, half,
                dma((dm,)), dma((dm,)), dma((dm,)), dma((dm,)), dma((dm,)), dma((dm,)),
                dma((2,)), dma((2,)), dma((2,)),
            ],
            compiler_params=pltpu.CompilerParams(has_side_effects=True),
        )(
            qm[0, 0], qm1[0, 0], qb[0, 0], energy_index[0, 0],
            codes[0], turner[None, :],
        )
        return tuple(out[None, None] for out in outs)

    return jax.shard_map(
        per_device,
        mesh=mesh,
        in_specs=(
            P("seq", "row", None, None, None),
            P("seq", "row", None, None, None),
            P("seq", "row", None, None, None),
            P("seq", "row", None),
            P("seq", "row", None, None),
            P(),
        ),
        out_specs=(
            P("seq", "row", None, None),
            P("seq", "row", None, None),
            P("seq", "row", None, None),
        ),
        check_vma=False,
    )
```

time: 713 us -> 45 us (0.06)
  local copies, waits for them, and re-layouts: 673 us -> 5.01 us
  Pallas kernels: 0 us -> 39.1 us
  matrix products: 12 us -> 0 us
  waiting for transfers between devices: 11.8 us -> 0 us
  starting transfers between devices: 10.5 us -> 0 us
    gather x2 -> x0, local copies, waits for them, and re-layouts: 670 us -> none  [per_device(): weight = jnp.exp(-jnp.take(turner, energy_index[0]))]
    pallas_call x0 -> x1, Pallas kernels: none -> 39.1 us  [per_device(): pl.pallas_call(functools.partial(kernel, plan, width), out_shape=[jax.Sha...]
    dot_general x25 -> x0, matrix products: 12 us -> none  [the longest x7 3.89 us: per_device(): tails = tails + jnp.dot(unpaired(shift), rights[shift - 1][0], precision=HI)]
    ppermute x8 -> x0, waiting for transfers between devices: 11.8 us -> none  [shifted(): return lax.ppermute(block, axis, route)]
    ppermute x8 -> x0, starting transfers between devices: 10.5 us -> none  [shifted(): return lax.ppermute(block, axis, route)]
  transfers between devices with their start and end apart: 8 -> 0, of which waited for: 3 -> 0; matrix products, arithmetic and copies ran while one was open for 95% -> 0% of each run, Pallas kernels for 0% -> 0%
where the time goes in v1:
time: 45 us; the launch traced here: 44.8 us
  Pallas kernels  39.1 us (87%)
  local copies, waits for them, and re-layouts  5.01 us (11%)
  between operations  0.64 us (1%)
    pallas_call x1, Pallas kernels, per_device(): pl.pallas_call(functools.partial(kernel, plan, width), out_shape=[jax.Sha...  39.1 us
    unnamed x3, local copies, waits for them, and re-layouts  5.01 us

profile of v1, /device:TPU:13, one launch (start us, length us, event | category | flops | bytes accessed | tf_op | source)
XLA Modules:
  0.0 44.8 jit_solution(4410846822065295746)
XLA Ops:
  0.6 39.1 %shard_map.85 = (f32[256,256]{1,0:T(8,128)}, f32[256,256]{1,0:T(8,128)}, f32[256,256]{1,0:T(8,128)}) custom-call(f32[7,256,256]{2,1,0:T(8,128)} %bitcast.9, f32[7,256,256]{2,1,0:T(8,128)} %bitcast.10, f32[7,256,256]{2,1,0:T(8,128)} %bitcast.11, s32[256,256]{1,0:T(8,128)} %bitcast.12, s32[1,256]{1,0:T(1,128)} %bitcast.16, f32[1,64]{1,0:T(1,128)} %bitcast.17), custom_call_target="tpu_custom_call" | custom-call | tf_op jit(solution)/shard_map/pallas_call | solution.py:286
  39.8 1.7 %copy.12 = f32[1,1,256,256]{3,2,1,0:T(8,128)} copy(f32[1,1,256,256]{3,2,1,0:T(8,128)} %bitcast.15) | data formatting | bytes 524288
  41.4 1.7 %copy.13 = f32[1,1,256,256]{3,2,1,0:T(8,128)} copy(f32[1,1,256,256]{3,2,1,0:T(8,128)} %bitcast.14) | data formatting | bytes 524288
  43.1 1.7 %copy.14 = f32[1,1,256,256]{3,2,1,0:T(8,128)} copy(f32[1,1,256,256]{3,2,1,0:T(8,128)} %bitcast.13) | data formatting | bytes 524288

commit v2 on v1

--- a/solution.py
+++ b/solution.py
@@ -11,13 +11,14 @@
 BF16 = jnp.bfloat16
 
 PLAN = {
-    1: (4, (3, 4, 5, 6, 7)),
-    3: (6, (1, 2, 3, 4, 5, 6, 7)),
-    4: (8, (4, 5, 6)),
-    5: (9, (3, 4, 5, 6, 7)),
-    6: (14, (3, 6, 7)),
-    7: (10, (1, 2, 3, 5, 6)),
+    1: (5, (3, 4, 5, 6, 7)),
+    3: (7, (1, 2, 3, 5, 6)),
+    4: (9, (5, 7)),
+    5: (8, (3, 4, 5, 6, 7)),
+    6: (10, (2, 3, 6, 7)),
+    7: (15, (1, 5, 6)),
 }
+CHUNKS = 4
 
 
 def split(x):
@@ -44,7 +45,7 @@
 
 def kernel(
     plan, width, qm, qm1, qb, eidx, codes, turner, pair_out, branch_out, multi_out,
-    q_own, r_own, q_far, r_far, qb_in, e_in, code_in, acc, acc_far, partial_in, weight, row_sum,
+    q_own, r_own, q_far, r_far, rf_h, rf_l, qb_in, e_in, code_in, acc, acc_far, partial_in, weight, row_sum,
     tri_h, tri_l, up_h, up_l,
     own_sem, q_send, q_recv, r_send, r_recv, rf_recv, load_sem, code_sem, part_sem,
 ):
@@ -77,8 +78,14 @@
     def code_send():
         return remote(codes, code_in, code_sem.at[0], code_sem.at[1], me - dist)
 
-    def q_copy(m, device):
-        return remote(qm.at[m - 1], q_far.at[m - 1], q_send.at[m - 1], q_recv.at[m - 1], device)
+    height = block // CHUNKS
+
+    def rows_of(c):
+        return pl.ds(c * height, height)
+
+    def q_copy(m, c, device):
+        at = (m - 1, rows_of(c))
+        return remote(qm.at[at], q_far.at[at], q_send.at[m - 1, c], q_recv.at[m - 1, c], device)
 
     def r_copy(m, device):
         return remote(qm1.at[dm - m], r_own.at[m - 1], r_send.at[m - 1], r_recv.at[m - 1], device)
@@ -86,17 +93,18 @@
     def rf_copy(m, device):
         return remote(qm1.at[dm - m], r_far.at[m - 1], r_send.at[m - 1], rf_recv.at[m - 1], device)
 
-    def part_copy(device):
-        return remote(acc_far, partial_in, part_sem.at[0], part_sem.at[1], device)
+    def part_copy(c, device):
+        at = pl.ds(c * height, height + (8 if c == CHUNKS - 1 else 0))
+        return remote(acc_far.at[at], partial_in.at[at], part_sem.at[0, c], part_sem.at[1, c], device)
+
+    @pl.when(me >= dist)
+    def _():
+        code_send().start()
 
     for m in range(1, dist):
         for row in moved_rows(m):
             device = plan[row][0]
 
-            @pl.when(me == row)
-            def _():
-                q_copy(m, device).start()
-
             if row + m == device:
 
                 @pl.when(me == device)
@@ -109,15 +117,19 @@
                 def _():
                     rf_copy(m, device).start()
 
+    for row, (device, shifts) in plan.items():
+
+        @pl.when(me == row)
+        def _():
+            for c in range(CHUNKS):
+                for m in shifts:
+                    q_copy(m, c, device).start()
+
     for m in range(1, dist):
 
         @pl.when(direct(m))
         def _():
             r_copy(m, me - m).start()
-
-    @pl.when(me >= dist)
-    def _():
-        code_send().start()
 
     loads = (
         pltpu.make_async_copy(qb, qb_in, load_sem.at[0]),
@@ -168,9 +180,7 @@
             total = total + qb_in[e - 1] * factor
         row_sum[...] = jnp.broadcast_to(jnp.sum(total, axis=1, keepdims=True), row_sum.shape)
 
-    def product(m, q, r, total):
-        right = r[m]
-        total[0:block, :] += dot3(split(q[m]), split(right))
+    def column_sum(m, right, total):
         fade = jnp.exp((-(m + 1) * block - column).astype(F32) * beta)
         total[block : block + 1, :] += jnp.sum(right * fade, axis=0, keepdims=True)
 
@@ -182,22 +192,28 @@
 
     if plan:
         far_mask = mask_of(list(plan.values()))
-
-        def far_step(m, rest):
-            @pl.when(rest % 2 == 1)
-            def _():
-                q_copy(m + 1, 0).wait_recv()
-                rf_copy(m + 1, 0).wait_recv()
-                product(m, q_far, r_far, acc_far)
-
-            return rest // 2
-
-        lax.fori_loop(0, dm, far_step, far_mask)
-        for row, (device, _) in plan.items():
-
-            @pl.when(me == device)
-            def _():
-                part_copy(row).start()
+        for c in range(CHUNKS):
+            at = rows_of(c)
+
+            def far_step(m, rest):
+                @pl.when(rest % 2 == 1)
+                def _():
+                    if c == 0:
+                        rf_copy(m + 1, 0).wait_recv()
+                        right = r_far[m]
+                        rf_h[m], rf_l[m] = split(right)
+                        column_sum(m, right, acc_far)
+                    q_copy(m + 1, c, 0).wait_recv()
+                    acc_far[at, :] += dot3(split(q_far[m, at, :]), (rf_h[m], rf_l[m]))
+
+                return rest // 2
+
+            lax.fori_loop(0, dm, far_step, far_mask)
+            for row, (device, _) in plan.items():
+
+                @pl.when(me == device)
+                def _():
+                    part_copy(c, row).start()
 
     moved = mask_of([(row, shifts) for row, (_, shifts) in plan.items()])
     own_mask = jnp.where(live, 2**dm - 1 - moved, 0)
@@ -207,7 +223,9 @@
         def _():
             pltpu.make_async_copy(qm.at[m], q_own.at[m], own_sem.at[m]).wait()
             r_copy(m + 1, 0).wait_recv()
-            product(m, q_own, r_own, acc)
+            right = r_own[m]
+            column_sum(m, right, acc)
+            acc[0:block, :] += dot3(split(q_own[m]), split(right))
 
         return rest // 2
 
@@ -217,7 +235,8 @@
 
         @pl.when(any_of(me, list(plan)))
         def _():
-            part_copy(0).wait_recv()
+            for c in range(CHUNKS):
+                part_copy(c, 0).wait_recv()
             acc[...] += partial_in[...]
 
     @pl.when(live)
@@ -231,11 +250,6 @@
         tails = 0.01 * jnp.exp(column.astype(F32) * beta) * acc[block : block + 1, :]
         multi_out[...] = summed + tails + dot3((up_h[...], up_l[...]), split(branch))
 
-    @pl.when(jnp.logical_not(live))
-    def _():
-        for out in (pair_out, branch_out, multi_out):
-            out[...] = jnp.zeros_like(out)
-
     for m in range(1, dist):
         rows = moved_rows(m)
         row = me - m
@@ -256,7 +270,8 @@
 
             @pl.when(any_of(me, rows))
             def _():
-                q_copy(m, 0).wait_send()
+                for c in range(CHUNKS):
+                    q_copy(m, c, 0).wait_send()
 
     @pl.when(me >= dist)
     def _():
@@ -266,7 +281,8 @@
 
         @pl.when(any_of(me, [device for device, _ in plan.values()]))
         def _():
-            part_copy(0).wait_send()
+            for c in range(CHUNKS):
+                part_copy(c, 0).wait_send()
 
 
 def solution(mesh):
@@ -277,6 +293,7 @@
         dist = dm + 1
         plan = PLAN if width == 16 and dist == 8 else {}
         blocks = pltpu.VMEM((dm, block, block), F32)
+        halves = pltpu.VMEM((dm, block, block), BF16)
         whole = pltpu.VMEM((block, block), F32)
         half = pltpu.VMEM((block, block), BF16)
         tall = pltpu.VMEM((block + 8, block), F32)
@@ -289,21 +306,22 @@
             in_specs=[anywhere] * 4 + [local] * 2,
             out_specs=[local] * 3,
             scratch_shapes=[
-                blocks, blocks, blocks, blocks, blocks,
+                blocks, blocks, blocks, blocks, halves, halves, blocks,
                 pltpu.VMEM((block, block), jnp.int32),
                 pltpu.VMEM((1, block), jnp.int32),
                 tall, tall, tall, whole,
                 pltpu.VMEM((block, 128), F32),
                 half, half, half, half,
-                dma((dm,)), dma((dm,)), dma((dm,)), dma((dm,)), dma((dm,)), dma((dm,)),
-                dma((2,)), dma((2,)), dma((2,)),
+                dma((dm,)), dma((dm, CHUNKS)), dma((dm, CHUNKS)), dma((dm,)), dma((dm,)), dma((dm,)),
+                dma((2,)), dma((2,)), dma((2, CHUNKS)),
             ],
             compiler_params=pltpu.CompilerParams(has_side_effects=True),
         )(
             qm[0, 0], qm1[0, 0], qb[0, 0], energy_index[0, 0],
             codes[0], turner[None, :],
         )
-        return tuple(out[None, None] for out in outs)
+        live = lax.axis_index("row") < width - dist
+        return tuple(jnp.where(live, out, 0.0)[None, None] for out in outs)
 
     return jax.shard_map(
         per_device,

time: 45 us -> 41.7 us (0.927)
  the two profiles are of different devices: /device:TPU:13 before, /device:TPU:12 now
where the time goes in v2:
time: 41.7 us; the launch traced here: 41.5 us
  Pallas kernels  37.3 us (89%)
  other arithmetic  3.53 us (8%)
  between operations  0.65 us (2%)
    pallas_call x1, Pallas kernels, per_device(): pl.pallas_call(functools.partial(kernel, plan, width), out_shape=[jax.Sha...  37.3 us
    broadcast_in_dim x2, other arithmetic, per_device(): return tuple((jnp.where(live, out, 0.0)[None, None] for out in outs))  3.53 us

profile of v2, /device:TPU:12, one launch (start us, length us, event | category | flops | bytes accessed | tf_op | source)
XLA Modules:
  0.0 41.5 jit_solution(8722779279224796584)
XLA Ops:
  0.6 37.3 %shard_map.85 = (f32[256,256]{1,0:T(8,128)}, f32[256,256]{1,0:T(8,128)}, f32[256,256]{1,0:T(8,128)}) custom-call(f32[7,256,256]{2,1,0:T(8,128)} %bitcast.12, f32[7,256,256]{2,1,0:T(8,128)} %bitcast.13, f32[7,256,256]{2,1,0:T(8,128)} %bitcast.14, s32[256,256]{1,0:T(8,128)} %bitcast.15, s32[1,256]{1,0:T(1,128)} %bitcast.16, f32[1,64]{1,0:T(1,128)} %bitcast.17), custom_call_target="tpu_custom_call" | custom-call | tf_op jit(solution)/shard_map/pallas_call | solution.py:303
  38.0 1.7 %select_bitcast_fusion.2 = f32[1,1,256,256]{3,2,1,0:T(8,128)} fusion(f32[256,256]{1,0:T(8,128)} %get-tuple-element.6, pred[]{:T(512)S(6)} %lt.3), kind=kLoop, calls=%fused_computation.2 | loop fusion | flops 65536 | bytes 524289 | tf_op jit(solution)/shard_map/broadcast_in_dim | solution.py:324
  39.6 1.9 %select_bitcast_fusion = (f32[1,1,256,256]{3,2,1,0:T(8,128)}, f32[1,1,256,256]{3,2,1,0:T(8,128)}) fusion(f32[256,256]{1,0:T(8,128)} %get-tuple-element.8, pred[]{:T(512)S(6)} %lt.3, f32[256,256]{1,0:T(8,128)} %get-tuple-element.7), kind=kLoop, calls=%fused_computation | loop fusion | flops 131072 | bytes 1048577 | tf_op jit(solution)/shard_map/broadcast_in_dim | solution.py:324

commit v3 on v2

--- a/solution.py
+++ b/solution.py
@@ -12,11 +12,11 @@
 
 PLAN = {
     1: (5, (3, 4, 5, 6, 7)),
-    3: (7, (1, 2, 3, 5, 6)),
-    4: (9, (5, 7)),
-    5: (8, (3, 4, 5, 6, 7)),
-    6: (10, (2, 3, 6, 7)),
-    7: (15, (1, 5, 6)),
+    2: (7, (2, 3, 4, 5, 6, 7)),
+    4: (9, (4, 5, 6, 7)),
+    5: (8, (3, 4, 6, 7)),
+    6: (11, (3, 6, 7)),
+    7: (10, (1, 2, 3, 5, 6)),
 }
 CHUNKS = 4
 
@@ -44,9 +44,8 @@
 
 
 def kernel(
-    plan, width, qm, qm1, qb, eidx, codes, turner, pair_out, branch_out, multi_out,
-    q_own, r_own, q_far, r_far, rf_h, rf_l, qb_in, e_in, code_in, acc, acc_far, partial_in, weight, row_sum,
-    tri_h, tri_l, up_h, up_l,
+    plan, width, qm, qm1, qb, eidx, codes, turner, acc, weight, row_sum,
+    q_own, r_own, q_far, r_far, rf_h, rf_l, qb_in, e_in, code_in, acc_far, partial_in,
     own_sem, q_send, q_recv, r_send, r_recv, rf_recv, load_sem, code_sem, part_sem,
 ):
     dm, block = qm.shape[0], qm.shape[1]
@@ -101,7 +100,7 @@
     def _():
         code_send().start()
 
-    for m in range(1, dist):
+    for m in range(dm, 0, -1):
         for row in moved_rows(m):
             device = plan[row][0]
 
@@ -122,10 +121,10 @@
         @pl.when(me == row)
         def _():
             for c in range(CHUNKS):
-                for m in shifts:
+                for m in reversed(shifts):
                     q_copy(m, c, device).start()
 
-    for m in range(1, dist):
+    for m in range(dm, 0, -1):
 
         @pl.when(direct(m))
         def _():
@@ -156,10 +155,6 @@
 
     @pl.when(live)
     def _():
-        diff = (cols_i - rows_i).astype(F32)
-        fall = jnp.where(diff >= 0, jnp.exp(diff * (-beta)), 0.0)
-        tri_h[...], tri_l[...] = split(fall)
-        up_h[...], up_l[...] = split(0.01 * fall)
         code_send().wait_recv()
         first = jnp.sum(jnp.where(rows_i == cols_i, codes[...].astype(F32), 0.0), axis=1, keepdims=True)
         both = first + code_in[...].astype(F32)
@@ -187,7 +182,7 @@
     def mask_of(cases):
         total = jnp.int32(0)
         for device, shifts in cases:
-            total = total + jnp.where(me == device, sum(2 ** (m - 1) for m in shifts), 0)
+            total = total + jnp.where(me == device, sum(2 ** (dm - m) for m in shifts), 0)
         return total
 
     if plan:
@@ -195,7 +190,9 @@
         for c in range(CHUNKS):
             at = rows_of(c)
 
-            def far_step(m, rest):
+            def far_step(step, rest):
+                m = dm - 1 - step
+
                 @pl.when(rest % 2 == 1)
                 def _():
                     if c == 0:
@@ -218,7 +215,9 @@
     moved = mask_of([(row, shifts) for row, (_, shifts) in plan.items()])
     own_mask = jnp.where(live, 2**dm - 1 - moved, 0)
 
-    def own_step(m, rest):
+    def own_step(step, rest):
+        m = dm - 1 - step
+
         @pl.when(rest % 2 == 1)
         def _():
             pltpu.make_async_copy(qm.at[m], q_own.at[m], own_sem.at[m]).wait()
@@ -239,17 +238,6 @@
                 part_copy(c, 0).wait_recv()
             acc[...] += partial_in[...]
 
-    @pl.when(live)
-    def _():
-        summed = acc[0:block, :]
-        pair = weight[...] * (1.0 + 0.8 * summed)
-        pair_out[...] = pair
-        outer = row_sum[:, 0:1] * jnp.exp(line.astype(F32) * (-beta))
-        branch = (outer + dot3(split(pair), (tri_h[...], tri_l[...]))) * beta
-        branch_out[...] = branch
-        tails = 0.01 * jnp.exp(column.astype(F32) * beta) * acc[block : block + 1, :]
-        multi_out[...] = summed + tails + dot3((up_h[...], up_l[...]), split(branch))
-
     for m in range(1, dist):
         rows = moved_rows(m)
         row = me - m
@@ -283,6 +271,35 @@
         def _():
             for c in range(CHUNKS):
                 part_copy(c, 0).wait_send()
+
+
+def finish(live_rows, dist, acc, weight, row_sum, pair_out, branch_out, multi_out):
+    block = weight.shape[0]
+    beta = 1.0 / (dist * block)
+    live = lax.axis_index("row") < live_rows
+
+    @pl.when(live)
+    def _():
+        column = lax.broadcasted_iota(jnp.int32, (block, 1), 0).astype(F32)
+        line = lax.broadcasted_iota(jnp.int32, (1, block), 1).astype(F32)
+        rows_i = lax.broadcasted_iota(jnp.int32, (block, block), 0)
+        cols_i = lax.broadcasted_iota(jnp.int32, (block, block), 1)
+        upper = jnp.where(cols_i >= rows_i, 1.0, 0.0).astype(BF16)
+        summed = acc[0:block, :]
+        pair = weight[...] * (1.0 + 0.8 * summed)
+        pair_out[...] = pair
+        high, low = split(pair * jnp.exp(line * beta))
+        inner = mm(high, upper) + mm(low, upper)
+        branch = (row_sum[:, 0:1] + inner) * (beta * jnp.exp(line * (-beta)))
+        branch_out[...] = branch
+        high, low = split(branch * jnp.exp(column * (-beta)))
+        tails = acc[block : block + 1, :] + mm(upper, high) + mm(upper, low)
+        multi_out[...] = summed + 0.01 * jnp.exp(column * beta) * tails
+
+    @pl.when(jnp.logical_not(live))
+    def _():
+        for out in (pair_out, branch_out, multi_out):
+            out[...] = jnp.zeros_like(out)
 
 
 def solution(mesh):
@@ -294,24 +311,25 @@
         plan = PLAN if width == 16 and dist == 8 else {}
         blocks = pltpu.VMEM((dm, block, block), F32)
         halves = pltpu.VMEM((dm, block, block), BF16)
-        whole = pltpu.VMEM((block, block), F32)
-        half = pltpu.VMEM((block, block), BF16)
+        square = jax.ShapeDtypeStruct((block, block), F32)
         tall = pltpu.VMEM((block + 8, block), F32)
         dma = pltpu.SemaphoreType.DMA
-        anywhere = pl.BlockSpec(memory_space=pl.ANY)
+        anywhere = pl.BlockSpec(memory_space=pltpu.HBM)
         local = pl.BlockSpec(memory_space=pltpu.VMEM)
-        outs = pl.pallas_call(
+        middle = pl.pallas_call(
             functools.partial(kernel, plan, width),
-            out_shape=[jax.ShapeDtypeStruct((block, block), F32)] * 3,
+            out_shape=[
+                pltpu.VMEM((block + 8, block), F32),
+                pltpu.VMEM((block, block), F32),
+                pltpu.VMEM((block, 128), F32),
+            ],
             in_specs=[anywhere] * 4 + [local] * 2,
             out_specs=[local] * 3,
             scratch_shapes=[
                 blocks, blocks, blocks, blocks, halves, halves, blocks,
                 pltpu.VMEM((block, block), jnp.int32),
                 pltpu.VMEM((1, block), jnp.int32),
-                tall, tall, tall, whole,
-                pltpu.VMEM((block, 128), F32),
-                half, half, half, half,
+                tall, tall,
                 dma((dm,)), dma((dm, CHUNKS)), dma((dm, CHUNKS)), dma((dm,)), dma((dm,)), dma((dm,)),
                 dma((2,)), dma((2,)), dma((2, CHUNKS)),
             ],
@@ -320,8 +338,14 @@
             qm[0, 0], qm1[0, 0], qb[0, 0], energy_index[0, 0],
             codes[0], turner[None, :],
         )
-        live = lax.axis_index("row") < width - dist
-        return tuple(jnp.where(live, out, 0.0)[None, None] for out in outs)
+        outs = pl.pallas_call(
+            functools.partial(finish, width - dist, dist),
+            out_shape=[square] * 3,
+            in_specs=[local] * 3,
+            out_specs=[local] * 3,
+            compiler_params=pltpu.CompilerParams(vmem_limit_bytes=16 * 2**20),
+        )(*middle)
+        return tuple(out[None, None] for out in outs)
 
     return jax.shard_map(
         per_device,

time: 41.7 us -> 38.9 us (0.933)
  the two profiles are of different devices: /device:TPU:12 before, /device:TPU:13 now
where the time goes in v3:
time: 38.9 us; the launch traced here: 38.7 us
  Pallas kernels  38.1 us (98%)
  between operations  0.64 us (2%)
    pallas_call x1, Pallas kernels, per_device(): pl.pallas_call(functools.partial(kernel, plan, width), out_shape=[pltpu.V...  36.6 us
    pallas_call x1, Pallas kernels, per_device(): pl.pallas_call(functools.partial(finish, width - dist, dist), out_shape=[...  1.44 us

profile of v3, /device:TPU:13, one launch (start us, length us, event | category | flops | bytes accessed | tf_op | source)
XLA Modules:
  0.0 38.7 jit_solution(14361033561589558846)
XLA Ops:
  0.6 36.6 %shard_map.85 = (f32[264,256]{1,0:T(8,128)S(1)}, f32[256,256]{1,0:T(8,128)S(1)}, f32[256,128]{1,0:T(8,128)S(1)}) custom-call(f32[7,256,256]{2,1,0:T(8,128)} %bitcast.9, f32[7,256,256]{2,1,0:T(8,128)} %bitcast.10, f32[7,256,256]{2,1,0:T(8,128)} %bitcast.11, s32[256,256]{1,0:T(8,128)} %bitcast.12, s32[1,256]{1,0:T(1,128)} %bitcast.13, f32[1,64]{1,0:T(1,128)} %bitcast.14), custom_call_target="tpu_custom_call" | custom-call | tf_op jit(solution)/shard_map/pallas_call | solution.py:319
  37.3 1.4 %shard_map.86 = (f32[256,256]{1,0:T(8,128)}, f32[256,256]{1,0:T(8,128)}, f32[256,256]{1,0:T(8,128)}) custom-call(f32[264,256]{1,0:T(8,128)S(1)} %get-tuple-element.9.acc, f32[256,256]{1,0:T(8,128)S(1)} %get-tuple-element.10.weight, f32[256,128]{1,0:T(8,128)S(1)} %get-tuple-element.11.row_sum), custom_call_target="tpu_custom_call" | custom-call | tf_op jit(solution)/shard_map/pallas_call | solution.py:341

commit v4 on v3

--- a/solution.py
+++ b/solution.py
@@ -12,11 +12,11 @@
 
 PLAN = {
     1: (5, (3, 4, 5, 6, 7)),
-    2: (7, (2, 3, 4, 5, 6, 7)),
-    4: (9, (4, 5, 6, 7)),
-    5: (8, (3, 4, 6, 7)),
-    6: (11, (3, 6, 7)),
-    7: (10, (1, 2, 3, 5, 6)),
+    2: (6, (2, 4, 5, 6, 7)),
+    4: (8, (4, 5, 6)),
+    5: (9, (3, 5, 6, 7)),
+    6: (10, (2, 3, 7)),
+    7: (15, (1, 2, 5, 6)),
 }
 CHUNKS = 4
 

time: 38.9 us -> 38 us (0.977)
  the two profiles are of different devices: /device:TPU:13 before, /device:TPU:8 now
where the time goes in v4:
time: 38 us; the launch traced here: 37.8 us
  Pallas kernels  37.2 us (98%)
  between operations  0.64 us (2%)
    pallas_call x1, Pallas kernels, per_device(): pl.pallas_call(functools.partial(kernel, plan, width), out_shape=[pltpu.V...  35.7 us
    pallas_call x1, Pallas kernels, per_device(): pl.pallas_call(functools.partial(finish, width - dist, dist), out_shape=[...  1.44 us

profile of v4, /device:TPU:8, one launch (start us, length us, event | category | flops | bytes accessed | tf_op | source)
XLA Modules:
  0.0 37.8 jit_solution(14030514147328342445)
XLA Ops:
  0.6 35.7 %shard_map.85 = (f32[264,256]{1,0:T(8,128)S(1)}, f32[256,256]{1,0:T(8,128)S(1)}, f32[256,128]{1,0:T(8,128)S(1)}) custom-call(f32[7,256,256]{2,1,0:T(8,128)} %bitcast.9, f32[7,256,256]{2,1,0:T(8,128)} %bitcast.10, f32[7,256,256]{2,1,0:T(8,128)} %bitcast.11, s32[256,256]{1,0:T(8,128)} %bitcast.12, s32[1,256]{1,0:T(1,128)} %bitcast.13, f32[1,64]{1,0:T(1,128)} %bitcast.14), custom_call_target="tpu_custom_call" | custom-call | tf_op jit(solution)/shard_map/pallas_call | solution.py:319
  36.4 1.4 %shard_map.86 = (f32[256,256]{1,0:T(8,128)}, f32[256,256]{1,0:T(8,128)}, f32[256,256]{1,0:T(8,128)}) custom-call(f32[264,256]{1,0:T(8,128)S(1)} %get-tuple-element.9.acc, f32[256,256]{1,0:T(8,128)S(1)} %get-tuple-element.10.weight, f32[256,128]{1,0:T(8,128)S(1)} %get-tuple-element.11.row_sum), custom_call_target="tpu_custom_call" | custom-call | tf_op jit(solution)/shard_map/pallas_call | solution.py:341

commit v5 on v4

--- a/solution.py
+++ b/solution.py
@@ -18,7 +18,7 @@
     6: (10, (2, 3, 7)),
     7: (15, (1, 2, 5, 6)),
 }
-CHUNKS = 4
+CHUNKS = 2
 
 
 def split(x):
@@ -95,6 +95,40 @@
     def part_copy(c, device):
         at = pl.ds(c * height, height + (8 if c == CHUNKS - 1 else 0))
         return remote(acc_far.at[at], partial_in.at[at], part_sem.at[0, c], part_sem.at[1, c], device)
+
+    barrier = pltpu.get_barrier_semaphore()
+
+    def greet(device):
+        pl.semaphore_signal(
+            barrier, inc=1, device_id={"row": device}, device_id_type=pl.DeviceIdType.MESH
+        )
+
+    extra = set()
+    for row, (device, shifts) in plan.items():
+        extra |= {(row, device), (device, row)} | {(row + m, device) for m in shifts}
+    extra = sorted((s, d) for s, d in extra if s != d and not (d < live_rows and 1 <= s - d <= dist))
+
+    @pl.when(live)
+    def _():
+        for m in range(1, dist + 1):
+            greet(me + m)
+
+    for source, device in extra:
+
+        @pl.when(me == device)
+        def _():
+            greet(source)
+
+    awaited = jnp.int32(0)
+    for m in range(1, dist + 1):
+        row = me - m
+        awaited = awaited + jnp.where(jnp.logical_and(row >= 0, row < live_rows), 1, 0)
+    for source, _ in extra:
+        awaited = awaited + jnp.where(me == source, 1, 0)
+
+    @pl.when(awaited > 0)
+    def _():
+        pl.semaphore_wait(barrier, awaited)
 
     @pl.when(me >= dist)
     def _():
@@ -333,7 +367,7 @@
                 dma((dm,)), dma((dm, CHUNKS)), dma((dm, CHUNKS)), dma((dm,)), dma((dm,)), dma((dm,)),
                 dma((2,)), dma((2,)), dma((2, CHUNKS)),
             ],
-            compiler_params=pltpu.CompilerParams(has_side_effects=True),
+            compiler_params=pltpu.CompilerParams(has_side_effects=True, collective_id=0),
         )(
             qm[0, 0], qm1[0, 0], qb[0, 0], energy_index[0, 0],
             codes[0], turner[None, :],

time: 38 us -> 33.8 us (0.89)
  Pallas kernels: 37.2 us -> 33 us
    pallas_call x1, Pallas kernels: 35.7 us -> 31.6 us  [per_device(): pl.pallas_call(functools.partial(kernel, plan, width), out_shape=[pltpu.V...]
where the time goes in v5:
time: 33.8 us; the launch traced here: 33.6 us
  Pallas kernels  33 us (98%)
  between operations  0.64 us (2%)
    pallas_call x1, Pallas kernels, per_device(): pl.pallas_call(functools.partial(kernel, plan, width), out_shape=[pltpu.V...  31.6 us
    pallas_call x1, Pallas kernels, per_device(): pl.pallas_call(functools.partial(finish, width - dist, dist), out_shape=[...  1.44 us

profile of v5, /device:TPU:8, one launch (start us, length us, event | category | flops | bytes accessed | tf_op | source)
XLA Modules:
  0.0 33.6 jit_solution(10473073273546287861)
XLA Ops:
  0.6 31.6 %shard_map.85 = (f32[264,256]{1,0:T(8,128)S(1)}, f32[256,256]{1,0:T(8,128)S(1)}, f32[256,128]{1,0:T(8,128)S(1)}) custom-call(f32[7,256,256]{2,1,0:T(8,128)} %bitcast.9, f32[7,256,256]{2,1,0:T(8,128)} %bitcast.10, f32[7,256,256]{2,1,0:T(8,128)} %bitcast.11, s32[256,256]{1,0:T(8,128)} %bitcast.12, s32[1,256]{1,0:T(1,128)} %bitcast.13, f32[1,64]{1,0:T(1,128)} %bitcast.14), custom_call_target="tpu_custom_call" | custom-call | tf_op jit(solution)/shard_map/pallas_call | solution.py:353
  32.2 1.4 %shard_map.86 = (f32[256,256]{1,0:T(8,128)}, f32[256,256]{1,0:T(8,128)}, f32[256,256]{1,0:T(8,128)}) custom-call(f32[264,256]{1,0:T(8,128)S(1)} %get-tuple-element.9.acc, f32[256,256]{1,0:T(8,128)S(1)} %get-tuple-element.10.weight, f32[256,128]{1,0:T(8,128)S(1)} %get-tuple-element.11.row_sum), custom_call_target="tpu_custom_call" | custom-call | tf_op jit(solution)/shard_map/pallas_call | solution.py:375
